TPU v7x, 512 devices: a whole 4x4x16 slice. The times are simulated.
512 devices in a mesh: gx: 128 (over x_lo, z, y), gy: 4 (over x_hi, core).
Axes of the slice: x: 4 (x_hi: 2, x_lo: 2; x = x_hi * 2 + x_lo), y: 4, z: 16, core: 2. Of those that a mesh axis runs over, the one named last changes fastest.
Arguments:
- populations: float32 [19, 1024, 64, 128], P(None, 'gx', 'gy'), as said below
- order_field: float32 [1024, 64, 128], P('gx', 'gy'), may hold values from -1 to 1
- solid_flags: int32 [1024, 64, 128], P('gx', 'gy'), may hold values 0 or 1
- plane_flags: int32 [128], replicated, may hold values 0 or 1
- shear_shift: int32 [1], replicated, may hold values from 1 to 63
- link_site: int32 [524288], P(('gx', 'gy')), may hold values from 0 to 16383, as said below
- link_dir: int32 [524288], P(('gx', 'gy')), may hold values from 1 to 18
- link_colloid: int32 [524288], P(('gx', 'gy')), may hold values from 0 to 2047
- link_count: int32 [4096], P(('gx', 'gy')), may hold values from 1 to 128, 327680 in all
- colloid_slot: int32 [2048], replicated, may hold values from 0 to 2047, each once
- colloid_speed: float32 [3, 2048], replicated, may hold values from -0.6 to 0.6
Outputs:
- new_populations: float32 [19, 1024, 64, 128], P(None, 'gx', 'gy')
- new_order: float32 [1024, 64, 128], P('gx', 'gy')
- colloid_force: float32 [3, 2048], P(None, ('gx', 'gy'))
Inputs may be any that keep to these rules, and one draw needn't show every extreme that they name: `populations`: populations lie between 0.2 w_i and 1.8 w_i. `link_site`: the slots of one device name distinct sites in rising order, one in each run of (8 * 16 * 128) / 1024 sites.
All inputs are finite; a program needn't handle non-finite values. No bound on the sum of `solid_flags` or of `link_count` on one device may be relied on, other than what follows from the above.
Results may differ from a plain program's by a relative error of at most 0.00002.
Values sent between devices are 32-bit elements; how exact they have to be, the bound alone decides.
A program may use at most 64 MiB of HBM per device.

v0:
```python
import jax
import jax.numpy as jnp
from jax import lax
from jax.sharding import PartitionSpec as P

VELOCITIES = [
    [0, 0, 0],
    [1, 0, 0],
    [-1, 0, 0],
    [0, 1, 0],
    [0, -1, 0],
    [0, 0, 1],
    [0, 0, -1],
    [1, 1, 0],
    [-1, -1, 0],
    [1, -1, 0],
    [-1, 1, 0],
    [1, 0, 1],
    [-1, 0, -1],
    [1, 0, -1],
    [-1, 0, 1],
    [0, 1, 1],
    [0, -1, -1],
    [0, 1, -1],
    [0, -1, 1],
]
WEIGHTS = [1.0 / 3.0] + [1.0 / 18.0] * 6 + [1.0 / 36.0] * 12
OPPOSITE = [0, 2, 1, 4, 3, 6, 5, 8, 7, 10, 9, 12, 11, 14, 13, 16, 15, 18, 17]
UP_X = [1, 7, 9, 11, 13]
DOWN_X = [2, 8, 10, 12, 14]
UP_Y = [3, 7, 10, 15, 17]
DOWN_Y = [4, 8, 9, 16, 18]
TAU = 0.8
BULK = 0.04
KAPPA = 0.04
MOBILITY = 0.2
PLANE_SPEED = 0.05


def padded_2(block, sides, width):
    for axis, dim in sides:
        count = lax.axis_size(axis)
        forward = [(i, i + 1) for i in range(count - 1)]
        forward.append((count - 1, 0))
        backward = [(target, source) for source, target in forward]
        low = lax.ppermute(
            lax.slice_in_dim(block, block.shape[dim] - width, None, axis=dim), axis, forward
        )
        high = lax.ppermute(lax.slice_in_dim(block, 0, width, axis=dim), axis, backward)
        block = jnp.concatenate([low, block, high], axis=dim)
    return block


def moments(stack):
    velocity_table = jnp.array(VELOCITIES, jnp.float32)
    shape = (19,) + (1,) * (stack.ndim - 1)
    density = jnp.sum(stack, axis=0)
    speed_x = jnp.sum(stack * velocity_table[:, 0].reshape(shape), axis=0) / density
    speed_y = jnp.sum(stack * velocity_table[:, 1].reshape(shape), axis=0) / density
    speed_z = jnp.sum(stack * velocity_table[:, 2].reshape(shape), axis=0) / density
    return (density, speed_x, speed_y, speed_z)


def boost_face(face, components, change):
    density, speed_x, speed_y, speed_z = moments(face)
    result = []
    for component in components:
        east_step, north_step, upward_step = VELOCITIES[component]
        weight = WEIGHTS[component]
        projection = east_step * speed_x + north_step * speed_y + upward_step * speed_z
        shifted = projection + north_step * change
        square_old = speed_x * speed_x + speed_y * speed_y + speed_z * speed_z
        moved_y = speed_y + change
        square_new = speed_x * speed_x + moved_y * moved_y + speed_z * speed_z
        correction = (
            weight
            * density
            * (
                3.0 * (shifted - projection)
                + 4.5 * (shifted * shifted - projection * projection)
                - 1.5 * (square_new - square_old)
            )
        )
        result.append(face[component] + correction)
    return jnp.stack(result)


def collide(read, force_x, force_y, force_z):
    velocity_table = jnp.array(VELOCITIES, jnp.float32)
    shape = (19,) + (1,) * (read.ndim - 1)
    density = jnp.sum(read, axis=0)
    speed_x = (
        jnp.sum(read * velocity_table[:, 0].reshape(shape), axis=0) + 0.5 * force_x
    ) / density
    speed_y = (
        jnp.sum(read * velocity_table[:, 1].reshape(shape), axis=0) + 0.5 * force_y
    ) / density
    speed_z = (
        jnp.sum(read * velocity_table[:, 2].reshape(shape), axis=0) + 0.5 * force_z
    ) / density
    square = speed_x * speed_x + speed_y * speed_y + speed_z * speed_z
    outputs = []
    for component in range(19):
        east_step, north_step, upward_step = VELOCITIES[component]
        weight = WEIGHTS[component]
        projection = east_step * speed_x + north_step * speed_y + upward_step * speed_z
        balance = (
            weight
            * density
            * (1.0 + 3.0 * projection + 4.5 * projection * projection - 1.5 * square)
        )
        along_force = east_step * force_x + north_step * force_y + upward_step * force_z
        forcing = weight * (
            3.0
            * (
                (east_step - speed_x) * force_x
                + (north_step - speed_y) * force_y
                + (upward_step - speed_z) * force_z
            )
            + 9.0 * projection * along_force
        )
        outputs.append(
            read[component] - (read[component] - balance) / TAU + (1.0 - 0.5 / TAU) * forcing
        )
    return (jnp.stack(outputs), speed_x, speed_y, speed_z)


def laplace(values):
    center = values[1:-1, 1:-1]
    return (
        values[2:, 1:-1]
        + values[:-2, 1:-1]
        + values[1:-1, 2:]
        + values[1:-1, :-2]
        + jnp.roll(center, -1, 2)
        + jnp.roll(center, 1, 2)
        - 6.0 * center
    )


def gradient(values):
    center = values[1:-1, 1:-1]
    return (
        (values[2:, 1:-1] - values[:-2, 1:-1]) * 0.5,
        (values[1:-1, 2:] - values[1:-1, :-2]) * 0.5,
        (jnp.roll(center, -1, 2) - jnp.roll(center, 1, 2)) * 0.5,
    )


def per_device(
    populations,
    order_field,
    solid_flags,
    plane_flags,
    shear_shift,
    link_site,
    link_dir,
    link_colloid,
    link_count,
    colloid_slot,
    colloid_speed,
):
    slab_index = lax.axis_index("gx")
    slab_count = lax.axis_size("gx")
    pencil_index = lax.axis_index("gy")
    pencil_count = lax.axis_size("gy")
    slab_depth, pencil_width, column_height = order_field.shape
    total_rows = pencil_width * pencil_count
    plane_shift = shear_shift[0]
    plane_low = plane_flags[slab_index]
    plane_high = plane_flags[(slab_index + 1) % slab_count]
    low_offset = plane_shift * plane_low
    high_offset = plane_shift * plane_high
    low_face = populations[:, 0]
    high_face = populations[:, slab_depth - 1]
    down_plain = jnp.stack([low_face[component] for component in DOWN_X])
    up_plain = jnp.stack([high_face[component] for component in UP_X])
    down_going = jnp.where(plane_low == 1, boost_face(low_face, DOWN_X, PLANE_SPEED), down_plain)
    up_going = jnp.where(plane_high == 1, boost_face(high_face, UP_X, -PLANE_SPEED), up_plain)
    low_message = jnp.concatenate([down_going, order_field[0:2]], axis=0)
    high_message = jnp.concatenate([up_going, order_field[slab_depth - 2 : slab_depth]], axis=0)

    def window(gathered, first_row):
        doubled = jnp.concatenate([gathered, gathered], axis=1)
        begin = jnp.mod(first_row, total_rows)
        return lax.dynamic_slice_in_dim(doubled, begin, pencil_width + 4, 1)

    packed = jnp.stack([low_message, high_message], axis=1)
    arrived = padded_2(packed, (("gx", 1),), 1)
    incoming = jnp.stack([arrived[:, 0], arrived[:, 3]], axis=0)
    gathered = lax.all_gather(incoming, "gy", axis=2, tiled=True)
    below = window(gathered[0], pencil_index * pencil_width - 2 - low_offset)
    above = window(gathered[1], pencil_index * pencil_width - 2 + high_offset)
    low_rows = jnp.concatenate(
        [
            jnp.stack([populations[component, :, 0] for component in DOWN_Y]),
            order_field[None, :, 0],
            order_field[None, :, 1],
        ],
        axis=0,
    )
    high_rows = jnp.concatenate(
        [
            jnp.stack([populations[component, :, pencil_width - 1] for component in UP_Y]),
            order_field[None, :, pencil_width - 2],
            order_field[None, :, pencil_width - 1],
        ],
        axis=0,
    )
    rims = padded_2(jnp.stack([low_rows, high_rows], axis=2), (("gy", 2),), 1)
    from_below = rims[:, :, 0]
    from_above = rims[:, :, 3]
    middle = jnp.concatenate(
        [
            from_below[5][:, None],
            from_below[6][:, None],
            order_field,
            from_above[5][:, None],
            from_above[6][:, None],
        ],
        axis=1,
    )
    padded = jnp.concatenate(
        [below[5][None], below[6][None], middle, above[5][None], above[6][None]], axis=0
    )
    inner_order = padded[1:-1, 1:-1]
    potential = BULK * (inner_order * inner_order * inner_order - inner_order) - KAPPA * laplace(
        padded
    )
    slope_x, slope_y, slope_z = gradient(potential)
    phase_x, phase_y, phase_z = gradient(inner_order)
    potential_curve = laplace(potential)
    zero_row = jnp.zeros((slab_depth, 1, column_height), jnp.float32)
    zero_layer = jnp.zeros((1, pencil_width + 2, column_height), jnp.float32)
    pieces = []
    for component in range(19):
        east_step, north_step, upward_step = VELOCITIES[component]
        low_row = from_below[UP_Y.index(component)][:, None] if north_step == 1 else zero_row
        high_row = from_above[DOWN_Y.index(component)][:, None] if north_step == -1 else zero_row
        extended = jnp.concatenate([low_row, populations[component], high_row], axis=1)
        left_layer = (
            below[UP_X.index(component), 1 : pencil_width + 3][None]
            if east_step == 1
            else zero_layer
        )
        right_layer = (
            above[DOWN_X.index(component), 1 : pencil_width + 3][None]
            if east_step == -1
            else zero_layer
        )
        extended = jnp.concatenate([left_layer, extended, right_layer], axis=0)
        pulled = extended[
            1 - east_step : 1 - east_step + slab_depth,
            1 - north_step : 1 - north_step + pencil_width,
        ]
        pieces.append(jnp.roll(pulled, upward_step, 2))
    read = jnp.stack(pieces)
    velocity_table = jnp.array(VELOCITIES, jnp.float32)
    weight_table = jnp.array(WEIGHTS, jnp.float32)
    opposite_table = jnp.array(OPPOSITE, jnp.int32)
    flat_stream = read.reshape((19, -1))
    flat_post = populations.reshape((19, -1))
    position = jnp.arange(link_site.shape[0], dtype=jnp.int32)
    live_links = position % 128 < link_count[position // 128]
    source = flat_post[link_dir, link_site]
    direction_vec = velocity_table[link_dir]
    link_weight = weight_table[link_dir]
    link_speed = colloid_speed[:, link_colloid]
    projection = jnp.sum(direction_vec.T * link_speed, axis=0)
    returned = source - 6.0 * link_weight * projection
    target = opposite_table[link_dir]
    current = flat_stream[target, link_site]
    flat_stream = flat_stream.at[target, link_site].set(jnp.where(live_links, returned, current))
    read = flat_stream.reshape(read.shape)
    transfer = (
        jnp.where(live_links, 2.0 * source - 6.0 * link_weight * projection, 0.0) * direction_vec.T
    )
    partial_value = jax.ops.segment_sum(
        transfer.T, colloid_slot[link_colloid], num_segments=colloid_slot.shape[0]
    ).T
    colloid_force = lax.psum_scatter(partial_value, ("gx", "gy"), scatter_dimension=1, tiled=True)
    collided, speed_x, speed_y, speed_z = collide(
        read, -order_field * slope_x, -order_field * slope_y, -order_field * slope_z
    )
    solid_mask = solid_flags == 1
    weight_shape = weight_table.reshape((19, 1, 1, 1))
    new_populations = jnp.where(solid_mask[None], weight_shape + 0.0 * collided, collided)
    advanced = (
        order_field
        - (speed_x * phase_x + speed_y * phase_y + speed_z * phase_z)
        + MOBILITY * potential_curve
    )
    new_order = jnp.where(solid_mask, order_field, advanced)
    return (new_populations, new_order, colloid_force)


def solution(mesh):
    return jax.shard_map(
        per_device,
        mesh=mesh,
        in_specs=(
            P(None, "gx", "gy", None),
            P("gx", "gy", None),
            P("gx", "gy", None),
            P(),
            P(),
            P(("gx", "gy")),
            P(("gx", "gy")),
            P(("gx", "gy")),
            P(("gx", "gy")),
            P(),
            P(),
        ),
        out_specs=(P(None, "gx", "gy", None), P("gx", "gy", None), P(None, ("gx", "gy"))),
        check_vma=False,
    )
```

profile of v0, /device:TPU:1, one launch (start us, length us, event | category | flops | bytes accessed | tf_op | source)
XLA Modules:
  0.0 232.4 jit_solution(17619595374594204179)
XLA Ops:
  0.7 1.0 bitcast_reduce_fusion
  1.7 0.9 slice_reduce_fusion
  2.7 0.7 fusion.273
  3.4 1.4 fusion.277
  5.4 1.1 fusion.4
  6.6 0.7 constant_dynamic-update-slice_fusion.9
  7.3 0.7 constant_dynamic-update-slice_fusion.8
  8.1 0.7 constant_dynamic-update-slice_fusion.7
  8.8 0.7 constant_dynamic-update-slice_fusion.6
  10.3 4.0 %collective-permute-start = (f32[7,1,16,128]{3,2,0,1:T(8,128)}, f32[7,1,16,128]{3,2,0,1:T(8,128)S(1)}, u32[]{:S(2)}, u32[]{:S(2)}) collective-permute-start(f32[7,1,16,128]{3,2,0,1:T(8,128)} %maximum_bitcast_fusion), channel_id=1, source_target_pairs={{0,4},{4,8},{8,12},{12,16},{16,20},{20,24},{24,28},{28,32},{32,36}... | collective-permute-start | bytes 172040 | tf_op jit(solution)/shard_map/ppermute | solution.py:46
  15.7 13.2 %collective-permute-start.1 = (f32[7,1,16,128]{3,2,0,1:T(8,128)}, f32[7,1,16,128]{3,2,0,1:T(8,128)}, u32[]{:S(2)}, u32[]{:S(2)}) collective-permute-start(f32[7,1,16,128]{3,2,0,1:T(8,128)} %maximum_bitcast_fusion.1), channel_id=1, source_target_pairs={{4,0},{8,4},{12,8},{16,12},{20,16},{24,20},{28,24},{32,28},{36,32}... | collective-permute-start | bytes 172040 | tf_op jit(solution)/shard_map/ppermute | solution.py:49
  33.1 5.2 %collective-permute-start.2 = (f32[7,8,1,128]{3,1,2,0:T(8,128)}, f32[7,8,1,128]{3,1,2,0:T(8,128)}, u32[]{:S(2)}, u32[]{:S(2)}) collective-permute-start(f32[7,8,1,128]{3,1,2,0:T(8,128)} %bitcast.45), channel_id=1, source_target_pairs={{0,1},{1,2},{2,3},{3,0},{4,5},{5,6},{6,7},{7,4},{8,9},{9,10},{10,1... | collective-permute-start | bytes 86024 | tf_op jit(solution)/shard_map/ppermute | solution.py:46
  42.4 1.9 collective-permute-start.3
  44.4 0.8 slice_bitcast_fusion.2
  47.5 0.9 copy.154
  48.9 8.6 %gather_fusion = f32[1024]{0:T(1024)S(1)} fusion(f32[19,16384]{1,0:T(8,128)S(1)} %bitcast.664, s32[1024]{0:T(1024)S(1)} %bitcast.582), kind=kCustom, calls=%fused_computation | custom fusion | bytes 16384 | tf_op jit(solution)/shard_map/gather | solution.py:265
  57.5 2.8 %gather_fusion.2 = f32[1024,3]{1,0:T(8,128)S(1)} fusion(f32[3,2048]{0,1:T(8,128)S(1)} %copy.134, s32[1024]{0:T(1024)S(1)} %get-tuple-element.192), kind=kCustom, calls=%fused_computation.2 | custom fusion | bytes 28672 | tf_op jit(solution)/shard_map/gather | solution.py:268
  60.3 2.8 %gather_fusion.1 = f32[1024,3]{1,0:T(8,128)S(1)} fusion(f32[19,3]{1,0:T(8,128)S(1)} %copy-done.1, s32[1024]{0:T(1024)S(1)} %get-tuple-element.162), kind=kCustom, calls=%fused_computation.1 | custom fusion | bytes 28672 | tf_op jit(solution)/shard_map/gather | solution.py:266
  63.4 4.3 %compare_select_fusion.2 = s32[1024,1]{0,1:T(1,128)S(1)} fusion(s32[]{:T(128)} %bitcast.109, s32[]{:T(128)} %bitcast.110, s32[]{:T(128)} %bitcast.111, s32[]{:T(128)} %bitcast.112, s32[]{:T(128)} %bitcast.113, s32[]{:T(128)} %bitcast.115, s32[]{:T(128)} %bitcast.114), kind=kLoop, calls=%fused_computation.412 | loop fusion | flops 23552 | bytes 4124 | tf_op jit(solution)/shard_map/gather | solution.py:264
  67.7 1.2 subtract_select_fusion
  70.5 6.2 %gather_fusion.4 = s32[1024]{0:T(1024)S(1)} fusion(s32[2048]{0:T(1024)S(1)} %copy-done, s32[1024]{0:T(1024)S(1)} %get-tuple-element.192), kind=kCustom, calls=%fused_computation.4 | custom fusion | bytes 12288 | tf_op jit(solution)/shard_map/gather | solution.py:279
  76.7 6.8 %scatter_custom_fusion = f32[2048,3]{1,0:T(8,128)S(1)} fusion(s32[1024]{0:T(1024)S(1)} %gather_fusion.4, f32[1024,3]{1,0:T(8,128)S(1)} %gather_fusion.1, f32[]{:T(128)} %constant.148.clone.1, f32[1024]{0:T(1024)S(1)} %get-tuple-element.26), kind=kCustom, calls=%fused_computation.12 | custom fusion | flops 6144 | bytes 552964 | tf_op jit(solution)/shard_map/scatter-add | solution.py:278
  83.5 104.1 %all-reduce = f32[3,2048]{0,1:T(8,128)S(1)} all-reduce(f32[3,2048]{0,1:T(8,128)S(1)} %bitcast.667), channel_id=2, replica_groups=mesh['gx'=128,'gy'=4] {'gx','gy'}, use_global_device_ids=true, to_apply=%region_15.16.clone | all-reduce | flops 6144 | bytes 49152
  194.2 0.7 fusion.194
  196.6 0.8 pad_maximum_fusion.9
  197.4 8.5 %all_gather.3 = f32[2,7,64,128]{3,2,1,0:T(8,128)S(1)} all-gather(f32[2,7,16,128]{3,2,1,0:T(8,128)S(1)} %pad_maximum_fusion.9), channel_id=1, replica_groups=mesh['gx'=128,'gy'=4] {'gy'}, dimensions={2}, use_global_device_ids=true | all-gather | bytes 573440 | tf_op jit(solution)/shard_map/all_gather | solution.py:191
  209.1 2.7 %stack.185 = f32[19,16384]{1,0:T(8,128)S(1)} concatenate(f32[1,16384]{1,0:T(1,128)S(1)} %bitcast.670, f32[1,16384]{1,0:T(1,128)S(1)} %bitcast.707, f32[1,16384]{1,0:T(1,128)S(1)} %bitcast.703, f32[1,16384]{1,0:T(1,128)} %bitcast.705, f32[1,16384]{1,0:T(1,128)} %bitcast.704, f32[1,16384]{1,0:T(1,128)S(1)} %bitcast.671, f32[1,16384]{1,0:T(1,128)S(1)} %bitcast.672, ...), dimensions={0} | concatenate | bytes 2490368 | tf_op jit(solution)/shard_map/stack | solution.py:257
  212.1 8.6 %gather_fusion.3 = f32[1024]{0:T(1024)S(1)} fusion(f32[19,16384]{1,0:T(8,128)S(1)} %stack.185, s32[1024]{0:T(1024)S(1)} %bitcast.583), kind=kCustom, calls=%fused_computation.3 | custom fusion | bytes 16384 | tf_op jit(solution)/shard_map/gather | solution.py:272
  220.7 5.0 %scatter_fusion = f32[311296]{0:T(1024)S(1)} fusion(f32[311296]{0:T(1024)S(1)} %reshape.949, s32[1024]{0:T(1024)S(1)} %copy-done.33, f32[1024]{0:T(1024)S(1)} %subtract_select_fusion.1), kind=kCustom, calls=%fused_computation.6 | custom fusion | bytes 16384
  226.7 1.0 multiply_reduce_fusion.1
  227.8 0.8 fusion.181
  231.1 1.2 add_select_fusion
  (200 shorter events, 26.8 us)
Async XLA Ops:
  0.6 69.9 %copy-start = (s32[2048]{0:T(1024)S(1)}, s32[2048]{0:T(1024)}, u32[]{:S(2)}) copy-start(s32[2048]{0:T(1024)} %param.26) | copy-start | bytes 24580
  0.6 8.9 %copy-start.2 = (f32[19,8,16,128]{3,2,1,0:T(8,128)S(1)}, f32[19,8,16,128]{3,2,1,0:T(8,128)}, u32[]{:S(2)}) copy-start(f32[19,8,16,128]{3,2,1,0:T(8,128)} %param.17) | copy-start | bytes 3735556
  0.7 28.3 %copy-start.3 = (f32[8,16,128]{2,1,0:T(8,128)S(1)}, f32[8,16,128]{2,1,0:T(8,128)}, u32[]{:S(2)}) copy-start(f32[8,16,128]{2,1,0:T(8,128)} %param.18) | copy-start | bytes 196612
  10.3 186.3 %collective-permute-start = (f32[7,1,16,128]{3,2,0,1:T(8,128)}, f32[7,1,16,128]{3,2,0,1:T(8,128)S(1)}, u32[]{:S(2)}, u32[]{:S(2)}) collective-permute-start(f32[7,1,16,128]{3,2,0,1:T(8,128)} %maximum_bitcast_fusion), channel_id=1, source_target_pairs={{0,4},{4,8},{8,12},{12,16},{16,20},{20,24},{24,28},{28,32},{32,36}... | collective-permute-start | bytes 172040 | tf_op jit(solution)/shard_map/ppermute | solution.py:46
  15.7 180.9 %collective-permute-start.1 = (f32[7,1,16,128]{3,2,0,1:T(8,128)}, f32[7,1,16,128]{3,2,0,1:T(8,128)}, u32[]{:S(2)}, u32[]{:S(2)}) collective-permute-start(f32[7,1,16,128]{3,2,0,1:T(8,128)} %maximum_bitcast_fusion.1), channel_id=1, source_target_pairs={{4,0},{8,4},{12,8},{16,12},{20,16},{24,20},{28,24},{32,28},{36,32}... | collective-permute-start | bytes 172040 | tf_op jit(solution)/shard_map/ppermute | solution.py:49
  33.1 158.0 %collective-permute-start.2 = (f32[7,8,1,128]{3,1,2,0:T(8,128)}, f32[7,8,1,128]{3,1,2,0:T(8,128)}, u32[]{:S(2)}, u32[]{:S(2)}) collective-permute-start(f32[7,8,1,128]{3,1,2,0:T(8,128)} %bitcast.45), channel_id=1, source_target_pairs={{0,1},{1,2},{2,3},{3,0},{4,5},{5,6},{6,7},{7,4},{8,9},{9,10},{10,1... | collective-permute-start | bytes 86024 | tf_op jit(solution)/shard_map/ppermute | solution.py:46
  42.4 149.4 %collective-permute-start.3 = (f32[7,8,1,128]{3,1,2,0:T(8,128)}, f32[7,8,1,128]{3,1,2,0:T(8,128)}, u32[]{:S(2)}, u32[]{:S(2)}) collective-permute-start(f32[7,8,1,128]{3,1,2,0:T(8,128)} %bitcast.58), channel_id=1, source_target_pairs={{1,0},{2,1},{3,2},{0,3},{5,4},{6,5},{7,6},{4,7},{9,8},{10,9},{11,1... | collective-permute-start | bytes 86024 | tf_op jit(solution)/shard_map/ppermute | solution.py:49
  44.4 2.3 copy-start.32
  44.4 2.9 %copy-start.38 = (s32[1024]{0:T(1024)S(1)}, s32[1024]{0:T(1024)}, u32[]{:S(2)}) copy-start(s32[1024]{0:T(1024)} %param.22) | copy-start | bytes 12292
  47.5 1.3 copy-start.34
  47.5 1.3 copy-start.36
  57.5 10.3 %copy-start.29 = (f32[1024]{0:T(1024)}, f32[1024]{0:T(1024)S(1)}, u32[]{:S(2)}) copy-start(f32[1024]{0:T(1024)S(1)} %gather_fusion) | copy-start | bytes 12292
  57.5 2.8 %copy-start.1 = (f32[19,3]{1,0:T(8,128)S(1)}, f32[19,3]{1,0:T(8,128)}, u32[]{:S(2)}) copy-start(f32[19,3]{1,0:T(8,128)} %constant.180.clone) | copy-start | bytes 688
  63.1 7.2 %copy-start.43 = (s32[2]{0:T(128)S(1)}, s32[2]{0:T(128)}, u32[]{:S(2)}) copy-start(s32[2]{0:T(128)} %constant.187) | copy-start | bytes 28
  63.1 7.3 %copy-start.42 = (s32[2]{0:T(128)S(1)}, s32[2]{0:T(128)}, u32[]{:S(2)}) copy-start(s32[2]{0:T(128)} %constant.190) | copy-start | bytes 28
  83.5 104.1 %copy-start.13 = (f32[8,16,1]{2,1,0:T(8,128)S(1)}, f32[8,16,1]{2,1,0:T(8,128)}, u32[]{:S(2)}) copy-start(f32[8,16,1]{2,1,0:T(8,128)} %slice.868) | copy-start | bytes 1540
  83.5 104.2 %copy-start.12 = (f32[8,16,127]{2,1,0:T(8,128)S(1)}, f32[8,16,127]{2,1,0:T(8,128)}, u32[]{:S(2)}) copy-start(f32[8,16,127]{2,1,0:T(8,128)} %slice.870) | copy-start | bytes 195076
  187.6 7.5 %copy-start.20 = (f32[8,16,128]{2,1,0:T(8,128)S(1)}, f32[8,16,128]{2,1,0:T(8,128)}, u32[]{:S(2)}) copy-start(f32[8,16,128]{2,1,0:T(8,128)} %get-tuple-element.81) | copy-start | bytes 196612
  187.6 7.5 %copy-start.21 = (f32[8,16,128]{2,1,0:T(8,128)S(1)}, f32[8,16,128]{2,1,0:T(8,128)}, u32[]{:S(2)}) copy-start(f32[8,16,128]{2,1,0:T(8,128)} %get-tuple-element.82) | copy-start | bytes 196612
  192.5 13.3 %copy-start.27 = (f32[1,8,1,128]{3,1,2,0:T(8,128)}, f32[1,8,1,128]{3,1,2,0:T(8,128)S(1)}, u32[]{:S(2)}) copy-start(f32[1,8,1,128]{3,1,2,0:T(8,128)S(1)} %get-tuple-element.147) | copy-start | bytes 12292
  206.2 1.7 copy-start.4
  206.2 1.7 copy-start.5
  206.2 1.7 copy-start.6
  206.2 1.7 copy-start.7
  212.0 8.6 %copy-start.30 = (f32[1024]{0:T(1024)S(1)}, f32[1024]{0:T(1024)}, u32[]{:S(2)}) copy-start(f32[1024]{0:T(1024)} %copy-done.29) | copy-start | bytes 12292
  212.1 8.6 %copy-start.35 = (f32[1024]{0:T(1024)S(1)}, f32[1024]{0:T(1024)}, u32[]{:S(2)}) copy-start(f32[1024]{0:T(1024)} %get-tuple-element.27) | copy-start | bytes 12292
  212.1 8.6 %copy-start.37 = (pred[1024]{0:T(1024)(128)(4,1)S(1)}, pred[1024]{0:T(1024)(128)(4,1)}, u32[]{:S(2)}) copy-start(pred[1024]{0:T(1024)(128)(4,1)} %get-tuple-element.28) | copy-start | bytes 3076
  212.1 8.7 %copy-start.33 = (s32[1024]{0:T(1024)S(1)}, s32[1024]{0:T(1024)}, u32[]{:S(2)}) copy-start(s32[1024]{0:T(1024)} %broadcast_select_fusion.2) | copy-start | bytes 12292
  226.7 1.1 copy-start.22
  226.7 1.1 copy-start.23
  226.7 1.1 copy-start.24
  226.7 1.1 copy-start.25
  (17 other events, 15.3 us)
where the time goes:
time: 233 us; the launch traced here: 232 us
  blocking collectives  113 us (48%)
  local copies, waits for them, and re-layouts  58.8 us (25%)
  other arithmetic  31.5 us (14%)
  starting transfers between devices  24.3 us (10%)
  between operations  5.2 us (2%)
    unnamed x1, blocking collectives  104 us
    unnamed x112, local copies, waits for them, and re-layouts  15.5 us
    ppermute x2, starting transfers between devices, padded_2(): lax.ppermute(lax.slice_in_dim(block, 0, width, axis=dim), axis, backward)  15.1 us
    ppermute x2, starting transfers between devices, padded_2(): lax.ppermute(lax.slice_in_dim(block, block.shape[dim] - width, None, axis...  9.21 us
    gather x1, local copies, waits for them, and re-layouts, per_device(): source = flat_post[link_dir, link_site]  8.59 us
    gather x1, local copies, waits for them, and re-layouts, per_device(): current = flat_stream[target, link_site]  8.59 us
    all_gather x1, blocking collectives, per_device(): gathered = lax.all_gather(incoming, 'gy', axis=2, tiled=True)  8.5 us
    scatter-add x1, other arithmetic, per_device(): jax.ops.segment_sum(transfer.T, colloid_slot[link_colloid], num_segments=...  6.8 us
  transfers between devices with their start and end apart: 4, of which 0 were waited for; matrix products, arithmetic and copies ran while one was open for 24% of the time, Pallas kernels for 0%

commit v1 on v0

--- a/solution.py
+++ b/solution.py
@@ -188,7 +188,9 @@
     packed = jnp.stack([low_message, high_message], axis=1)
     arrived = padded_2(packed, (("gx", 1),), 1)
     incoming = jnp.stack([arrived[:, 0], arrived[:, 3]], axis=0)
-    gathered = lax.all_gather(incoming, "gy", axis=2, tiled=True)
+    gathered = jnp.concatenate(
+        lax.all_to_all(jnp.stack([incoming] * lax.axis_size("gy")), "gy", 0, 0), axis=2
+    )
     below = window(gathered[0], pencil_index * pencil_width - 2 - low_offset)
     above = window(gathered[1], pencil_index * pencil_width - 2 + high_offset)
     low_rows = jnp.concatenate(

time: 233 us -> 235 us (level)
  blocking collectives: 113 us -> 104 us
  waiting for transfers between devices: 0.01 us -> 6.38 us
  starting transfers between devices: 24.3 us -> 28.6 us
    all_gather x1 -> x0, blocking collectives: 8.5 us -> none  [per_device(): gathered = lax.all_gather(incoming, 'gy', axis=2, tiled=True)]
    all_to_all x0 -> x1, waiting for transfers between devices: none -> 6.37 us  [per_device(): lax.all_to_all(jnp.stack([incoming] * lax.axis_size('gy')), 'gy', 0, 0)]
    all_to_all x0 -> x1, starting transfers between devices: none -> 4.28 us  [per_device(): lax.all_to_all(jnp.stack([incoming] * lax.axis_size('gy')), 'gy', 0, 0)]
    unnamed x112 -> x108, local copies, waits for them, and re-layouts: 15.5 us -> 15.4 us
  transfers between devices with their start and end apart: 4 -> 5, of which waited for: 0 -> 1; matrix products, arithmetic and copies ran while one was open for 24% -> 23% of each run, Pallas kernels for 0% -> 0%
where the time goes in v1:
time: 235 us; the launch traced here: 234 us
  blocking collectives  104 us (44%)
  local copies, waits for them, and re-layouts  59.5 us (25%)
  other arithmetic  30.4 us (13%)
  starting transfers between devices  28.6 us (12%)
  waiting for transfers between devices  6.38 us (3%)
  between operations  4.94 us (2%)
    unnamed x1, blocking collectives  104 us
    unnamed x108, local copies, waits for them, and re-layouts  15.4 us
    ppermute x2, starting transfers between devices, padded_2(): lax.ppermute(lax.slice_in_dim(block, 0, width, axis=dim), axis, backward)  15.1 us
    ppermute x2, starting transfers between devices, padded_2(): lax.ppermute(lax.slice_in_dim(block, block.shape[dim] - width, None, axis...  9.21 us
    gather x1, local copies, waits for them, and re-layouts, per_device(): source = flat_post[link_dir, link_site]  8.59 us
    gather x1, local copies, waits for them, and re-layouts, per_device(): current = flat_stream[target, link_site]  8.59 us
    scatter-add x1, other arithmetic, per_device(): jax.ops.segment_sum(transfer.T, colloid_slot[link_colloid], num_segments=...  6.8 us
    all_to_all x1, waiting for transfers between devices, per_device(): lax.all_to_all(jnp.stack([incoming] * lax.axis_size('gy')), 'gy', 0, 0)  6.37 us
  transfers between devices with their start and end apart: 5, of which 1 were waited for; matrix products, arithmetic and copies ran while one was open for 23% of the time, Pallas kernels for 0%

profile of v1, /device:TPU:1, one launch (start us, length us, event | category | flops | bytes accessed | tf_op | source)
XLA Modules:
  0.0 233.9 jit_solution(934361544118235824)
XLA Ops:
  0.7 1.0 bitcast_reduce_fusion
  1.7 0.9 slice_reduce_fusion
  3.4 1.3 fusion.278
  5.4 1.1 fusion.4
  6.5 0.7 constant_dynamic-update-slice_fusion.9
  7.3 0.7 constant_dynamic-update-slice_fusion.8
  8.0 0.7 constant_dynamic-update-slice_fusion.7
  8.8 0.7 constant_dynamic-update-slice_fusion.6
  10.2 4.0 %collective-permute-start = (f32[7,1,16,128]{3,2,0,1:T(8,128)}, f32[7,1,16,128]{3,2,0,1:T(8,128)S(1)}, u32[]{:S(2)}, u32[]{:S(2)}) collective-permute-start(f32[7,1,16,128]{3,2,0,1:T(8,128)} %maximum_bitcast_fusion), channel_id=1, source_target_pairs={{0,4},{4,8},{8,12},{12,16},{16,20},{20,24},{24,28},{28,32},{32,36}... | collective-permute-start | bytes 172040 | tf_op jit(solution)/shard_map/ppermute | solution.py:46
  15.5 13.2 %collective-permute-start.1 = (f32[7,1,16,128]{3,2,0,1:T(8,128)}, f32[7,1,16,128]{3,2,0,1:T(8,128)}, u32[]{:S(2)}, u32[]{:S(2)}) collective-permute-start(f32[7,1,16,128]{3,2,0,1:T(8,128)} %maximum_bitcast_fusion.1), channel_id=1, source_target_pairs={{4,0},{8,4},{12,8},{16,12},{20,16},{24,20},{28,24},{32,28},{36,32}... | collective-permute-start | bytes 172040 | tf_op jit(solution)/shard_map/ppermute | solution.py:49
  32.9 5.2 %collective-permute-start.2 = (f32[7,8,1,128]{3,1,2,0:T(8,128)}, f32[7,8,1,128]{3,1,2,0:T(8,128)}, u32[]{:S(2)}, u32[]{:S(2)}) collective-permute-start(f32[7,8,1,128]{3,1,2,0:T(8,128)} %bitcast.46), channel_id=1, source_target_pairs={{0,1},{1,2},{2,3},{3,0},{4,5},{5,6},{6,7},{7,4},{8,9},{9,10},{10,1... | collective-permute-start | bytes 86024 | tf_op jit(solution)/shard_map/ppermute | solution.py:46
  42.2 1.9 collective-permute-start.3
  44.2 0.8 slice_bitcast_fusion
  47.3 0.9 copy.186
  48.6 8.6 %gather_fusion = f32[1024]{0:T(1024)S(1)} fusion(f32[19,16384]{1,0:T(8,128)S(1)} %bitcast.665, s32[1024]{0:T(1024)S(1)} %bitcast.583), kind=kCustom, calls=%fused_computation | custom fusion | bytes 16384 | tf_op jit(solution)/shard_map/gather | solution.py:267
  57.3 2.8 %gather_fusion.2 = f32[1024,3]{1,0:T(8,128)S(1)} fusion(f32[3,2048]{0,1:T(8,128)S(1)} %copy.166, s32[1024]{0:T(1024)S(1)} %get-tuple-element.198), kind=kCustom, calls=%fused_computation.2 | custom fusion | bytes 28672 | tf_op jit(solution)/shard_map/gather | solution.py:270
  60.1 2.8 %gather_fusion.1 = f32[1024,3]{1,0:T(8,128)S(1)} fusion(f32[19,3]{1,0:T(8,128)S(1)} %copy-done.1, s32[1024]{0:T(1024)S(1)} %get-tuple-element.165), kind=kCustom, calls=%fused_computation.1 | custom fusion | bytes 28672 | tf_op jit(solution)/shard_map/gather | solution.py:268
  63.1 4.4 %compare_select_fusion.2 = s32[1024,1]{0,1:T(1,128)S(1)} fusion(s32[]{:T(128)} %bitcast.110, s32[]{:T(128)} %bitcast.111, s32[]{:T(128)} %bitcast.112, s32[]{:T(128)} %bitcast.113, s32[]{:T(128)} %bitcast.114, s32[]{:T(128)} %bitcast.116, s32[]{:T(128)} %bitcast.115), kind=kLoop, calls=%fused_computation.411 | loop fusion | flops 23552 | bytes 4124 | tf_op jit(solution)/shard_map/gather | solution.py:266
  67.5 1.3 subtract_select_fusion
  70.5 6.2 %gather_fusion.4 = s32[1024]{0:T(1024)S(1)} fusion(s32[2048]{0:T(1024)S(1)} %copy-done, s32[1024]{0:T(1024)S(1)} %get-tuple-element.198), kind=kCustom, calls=%fused_computation.4 | custom fusion | bytes 12288 | tf_op jit(solution)/shard_map/gather | solution.py:281
  76.6 6.8 %scatter_custom_fusion = f32[2048,3]{1,0:T(8,128)S(1)} fusion(s32[1024]{0:T(1024)S(1)} %gather_fusion.4, f32[1024,3]{1,0:T(8,128)S(1)} %gather_fusion.1, f32[]{:T(128)} %constant.148.clone.1, f32[1024]{0:T(1024)S(1)} %get-tuple-element.29), kind=kCustom, calls=%fused_computation.12 | custom fusion | flops 6144 | bytes 552964 | tf_op jit(solution)/shard_map/scatter-add | solution.py:280
  83.5 104.1 %all-reduce = f32[3,2048]{0,1:T(8,128)S(1)} all-reduce(f32[3,2048]{0,1:T(8,128)S(1)} %bitcast.668), channel_id=2, replica_groups=mesh['gx'=128,'gy'=4] {'gx','gy'}, use_global_device_ids=true, to_apply=%region_15.16.clone | all-reduce | flops 6144 | bytes 49152
  192.7 0.9 pad_maximum_fusion.9
  193.6 0.8 stack.172
  194.4 4.3 %all-to-all-start = ((f32[4,2,7,16,128]{4,3,2,1,0:T(8,128)}), f32[4,2,7,16,128]{4,3,2,1,0:T(8,128)S(1)}, u32[]{:S(2)}, u32[]{:S(2)}) async-start(f32[4,2,7,16,128]{4,3,2,1,0:T(8,128)} %stack.172), calls=%async_computation | async-start | bytes 917504 | tf_op jit(solution)/shard_map/all_to_all | solution.py:192
  201.1 6.4 %all-to-all-done = f32[4,2,7,16,128]{4,3,2,1,0:T(8,128)S(1)} async-done(((f32[4,2,7,16,128]{4,3,2,1,0:T(8,128)}), f32[4,2,7,16,128]{4,3,2,1,0:T(8,128)S(1)}, u32[]{:S(2)}, u32[]{:S(2)}) %all-to-all-start) | async-done | bytes 458784 | tf_op jit(solution)/shard_map/all_to_all | solution.py:192
  210.6 2.7 %stack.193 = f32[19,16384]{1,0:T(8,128)S(1)} concatenate(f32[1,16384]{1,0:T(1,128)S(1)} %bitcast.674, f32[1,16384]{1,0:T(1,128)S(1)} %bitcast.711, f32[1,16384]{1,0:T(1,128)S(1)} %bitcast.707, f32[1,16384]{1,0:T(1,128)} %bitcast.709, f32[1,16384]{1,0:T(1,128)} %bitcast.708, f32[1,16384]{1,0:T(1,128)S(1)} %bitcast.675, f32[1,16384]{1,0:T(1,128)S(1)} %bitcast.676, ...), dimensions={0} | concatenate | bytes 2490368 | tf_op jit(solution)/shard_map/stack | solution.py:259
  213.6 8.6 %gather_fusion.3 = f32[1024]{0:T(1024)S(1)} fusion(f32[19,16384]{1,0:T(8,128)S(1)} %stack.193, s32[1024]{0:T(1024)S(1)} %bitcast.584), kind=kCustom, calls=%fused_computation.3 | custom fusion | bytes 16384 | tf_op jit(solution)/shard_map/gather | solution.py:274
  222.3 5.0 %scatter_fusion = f32[311296]{0:T(1024)S(1)} fusion(f32[311296]{0:T(1024)S(1)} %reshape.960, s32[1024]{0:T(1024)S(1)} %copy-done.31, f32[1024]{0:T(1024)S(1)} %subtract_select_fusion.1), kind=kCustom, calls=%fused_computation.6 | custom fusion | bytes 16384
  228.3 1.0 multiply_reduce_fusion.1
  229.3 0.8 fusion.181
  232.7 1.2 add_select_fusion
  (199 shorter events, 27.0 us)
Async XLA Ops:
  0.6 69.8 %copy-start = (s32[2048]{0:T(1024)S(1)}, s32[2048]{0:T(1024)}, u32[]{:S(2)}) copy-start(s32[2048]{0:T(1024)} %param.26) | copy-start | bytes 24580
  0.6 8.9 %copy-start.2 = (f32[19,8,16,128]{3,2,1,0:T(8,128)S(1)}, f32[19,8,16,128]{3,2,1,0:T(8,128)}, u32[]{:S(2)}) copy-start(f32[19,8,16,128]{3,2,1,0:T(8,128)} %param.17) | copy-start | bytes 3735556
  0.7 28.1 %copy-start.3 = (f32[8,16,128]{2,1,0:T(8,128)S(1)}, f32[8,16,128]{2,1,0:T(8,128)}, u32[]{:S(2)}) copy-start(f32[8,16,128]{2,1,0:T(8,128)} %param.18) | copy-start | bytes 196612
  10.2 182.5 %collective-permute-start = (f32[7,1,16,128]{3,2,0,1:T(8,128)}, f32[7,1,16,128]{3,2,0,1:T(8,128)S(1)}, u32[]{:S(2)}, u32[]{:S(2)}) collective-permute-start(f32[7,1,16,128]{3,2,0,1:T(8,128)} %maximum_bitcast_fusion), channel_id=1, source_target_pairs={{0,4},{4,8},{8,12},{12,16},{16,20},{20,24},{24,28},{28,32},{32,36}... | collective-permute-start | bytes 172040 | tf_op jit(solution)/shard_map/ppermute | solution.py:46
  15.5 177.2 %collective-permute-start.1 = (f32[7,1,16,128]{3,2,0,1:T(8,128)}, f32[7,1,16,128]{3,2,0,1:T(8,128)}, u32[]{:S(2)}, u32[]{:S(2)}) collective-permute-start(f32[7,1,16,128]{3,2,0,1:T(8,128)} %maximum_bitcast_fusion.1), channel_id=1, source_target_pairs={{4,0},{8,4},{12,8},{16,12},{20,16},{24,20},{28,24},{32,28},{36,32}... | collective-permute-start | bytes 172040 | tf_op jit(solution)/shard_map/ppermute | solution.py:49
  32.9 158.0 %collective-permute-start.2 = (f32[7,8,1,128]{3,1,2,0:T(8,128)}, f32[7,8,1,128]{3,1,2,0:T(8,128)}, u32[]{:S(2)}, u32[]{:S(2)}) collective-permute-start(f32[7,8,1,128]{3,1,2,0:T(8,128)} %bitcast.46), channel_id=1, source_target_pairs={{0,1},{1,2},{2,3},{3,0},{4,5},{5,6},{6,7},{7,4},{8,9},{9,10},{10,1... | collective-permute-start | bytes 86024 | tf_op jit(solution)/shard_map/ppermute | solution.py:46
  42.2 149.4 %collective-permute-start.3 = (f32[7,8,1,128]{3,1,2,0:T(8,128)}, f32[7,8,1,128]{3,1,2,0:T(8,128)}, u32[]{:S(2)}, u32[]{:S(2)}) collective-permute-start(f32[7,8,1,128]{3,1,2,0:T(8,128)} %bitcast.59), channel_id=1, source_target_pairs={{1,0},{2,1},{3,2},{0,3},{5,4},{6,5},{7,6},{4,7},{9,8},{10,9},{11,1... | collective-permute-start | bytes 86024 | tf_op jit(solution)/shard_map/ppermute | solution.py:49
  44.2 2.2 copy-start.30
  44.2 2.9 %copy-start.36 = (s32[1024]{0:T(1024)S(1)}, s32[1024]{0:T(1024)}, u32[]{:S(2)}) copy-start(s32[1024]{0:T(1024)} %param.22) | copy-start | bytes 12292
  47.3 1.3 copy-start.32
  47.3 1.3 copy-start.34
  57.2 10.3 %copy-start.27 = (f32[1024]{0:T(1024)}, f32[1024]{0:T(1024)S(1)}, u32[]{:S(2)}) copy-start(f32[1024]{0:T(1024)S(1)} %gather_fusion) | copy-start | bytes 12292
  57.2 2.8 %copy-start.1 = (f32[19,3]{1,0:T(8,128)S(1)}, f32[19,3]{1,0:T(8,128)}, u32[]{:S(2)}) copy-start(f32[19,3]{1,0:T(8,128)} %constant.180.clone) | copy-start | bytes 688
  62.9 7.4 %copy-start.41 = (s32[2]{0:T(128)S(1)}, s32[2]{0:T(128)}, u32[]{:S(2)}) copy-start(s32[2]{0:T(128)} %constant.187) | copy-start | bytes 28
  62.9 7.4 %copy-start.40 = (s32[2]{0:T(128)S(1)}, s32[2]{0:T(128)}, u32[]{:S(2)}) copy-start(s32[2]{0:T(128)} %constant.190) | copy-start | bytes 28
  83.4 104.1 %copy-start.11 = (f32[8,16,1]{2,1,0:T(8,128)S(1)}, f32[8,16,1]{2,1,0:T(8,128)}, u32[]{:S(2)}) copy-start(f32[8,16,1]{2,1,0:T(8,128)} %slice.870) | copy-start | bytes 1540
  83.4 104.2 %copy-start.10 = (f32[8,16,127]{2,1,0:T(8,128)S(1)}, f32[8,16,127]{2,1,0:T(8,128)}, u32[]{:S(2)}) copy-start(f32[8,16,127]{2,1,0:T(8,128)} %slice.872) | copy-start | bytes 195076
  192.3 6.4 %copy-start.25 = (f32[1,8,1,128]{3,1,2,0:T(8,128)}, f32[1,8,1,128]{3,1,2,0:T(8,128)S(1)}, u32[]{:S(2)}) copy-start(f32[1,8,1,128]{3,1,2,0:T(8,128)S(1)} %get-tuple-element.150) | copy-start | bytes 12292
  192.7 7.7 %copy-start.18 = (f32[8,16,128]{2,1,0:T(8,128)S(1)}, f32[8,16,128]{2,1,0:T(8,128)}, u32[]{:S(2)}) copy-start(f32[8,16,128]{2,1,0:T(8,128)} %get-tuple-element.84) | copy-start | bytes 196612
  192.7 7.7 %copy-start.19 = (f32[8,16,128]{2,1,0:T(8,128)S(1)}, f32[8,16,128]{2,1,0:T(8,128)}, u32[]{:S(2)}) copy-start(f32[8,16,128]{2,1,0:T(8,128)} %get-tuple-element.85) | copy-start | bytes 196612
  194.4 13.1 %all-to-all-start = ((f32[4,2,7,16,128]{4,3,2,1,0:T(8,128)}), f32[4,2,7,16,128]{4,3,2,1,0:T(8,128)S(1)}, u32[]{:S(2)}, u32[]{:S(2)}) async-start(f32[4,2,7,16,128]{4,3,2,1,0:T(8,128)} %stack.172), calls=%async_computation | async-start | bytes 917504 | tf_op jit(solution)/shard_map/all_to_all | solution.py:192
  207.8 1.7 copy-start.4
  207.8 1.7 copy-start.5
  207.8 1.7 copy-start.6
  207.8 1.7 copy-start.7
  213.6 8.6 %copy-start.28 = (f32[1024]{0:T(1024)S(1)}, f32[1024]{0:T(1024)}, u32[]{:S(2)}) copy-start(f32[1024]{0:T(1024)} %copy-done.27) | copy-start | bytes 12292
  213.6 8.6 %copy-start.33 = (f32[1024]{0:T(1024)S(1)}, f32[1024]{0:T(1024)}, u32[]{:S(2)}) copy-start(f32[1024]{0:T(1024)} %get-tuple-element.30) | copy-start | bytes 12292
  213.6 8.6 %copy-start.35 = (pred[1024]{0:T(1024)(128)(4,1)S(1)}, pred[1024]{0:T(1024)(128)(4,1)}, u32[]{:S(2)}) copy-start(pred[1024]{0:T(1024)(128)(4,1)} %get-tuple-element.31) | copy-start | bytes 3076
  213.6 8.7 %copy-start.31 = (s32[1024]{0:T(1024)S(1)}, s32[1024]{0:T(1024)}, u32[]{:S(2)}) copy-start(s32[1024]{0:T(1024)} %broadcast_select_fusion.2) | copy-start | bytes 12292
  228.2 1.1 copy-start.20
  228.2 1.1 copy-start.21
  228.2 1.1 copy-start.22
  (16 other events, 14.6 us)
